TPU v7x, 32 devices: a whole 2x2x4 slice. The times are simulated.
32 devices in a mesh: rows: 8 (over y, x, core), sub: 4 (over z).
Axes of the slice: x: 2, y: 2, z: 4, core: 2. Of those that a mesh axis runs over, the one named last changes fastest.
Arguments:
- old_basis: bfloat16 [32, 524288], P(None, ('rows', 'sub')), may hold values from -1 to 1
- snapshots: bfloat16 [512, 524288], P(None, ('rows', 'sub')), may hold values from -16 to 16
- gap_flags: int32 [512, 4096], P(None, ('rows', 'sub')), may hold values from 0 to 1, as said below
- sketch_seed: int32 [512, 64], replicated, may hold values from -1 to 1
Outputs:
- new_basis: float32 [32, 524288], P(None, ('rows', 'sub'))
- coefficients: float32 [32, 512], replicated
Inputs may be any that keep to these rules, and one draw needn't show every extreme that they name: `gap_flags`: 1 marks a block of 128 velocity rows measured in that snapshot, 0 a gap; every snapshot has measured blocks and gaps.
All inputs are finite; a program needn't handle non-finite values.
Results may differ from a plain program's by a relative error of at most 0.00135.
The roundings to bfloat16 on the way count: a program that leaves them out, or rounds other values in their place, can miss the bound.
Values may be sent and summed in bfloat16 or wider, within the bound.
No kernel may reach another device: no remote copies, remote signals or barrier semaphores. Data moves between devices by JAX's collectives and lax.ppermute only.
A program may use at most 192 MiB of HBM per device.

v0:
```python
import math
import jax
import jax.numpy as jnp
from jax import lax
from jax.sharding import PartitionSpec as P

POWER = 2
damping = 0.005
highest = lax.Precision.HIGHEST


def cholesky_last(system):
    extent = system.shape[0]
    factor = jnp.zeros_like(system)
    for column in range(extent):
        partial_sum = jnp.sum(factor * factor[column : column + 1], axis=1)
        remain = system[:, column] - partial_sum
        diagonal_root = jnp.sqrt(remain[column])
        lower_part = (jnp.arange(extent) >= column).reshape((extent,) + (1,) * (system.ndim - 2))
        factor = factor.at[:, column].set(jnp.where(lower_part, remain / diagonal_root, 0.0))
    return factor


def lower_solve(factor, target):
    extent = factor.shape[0]
    result = jnp.zeros_like(target)
    for column in range(extent):
        current = (target[column] - jnp.sum(factor[column] * result, axis=0)) / factor[
            column, column
        ]
        result = result.at[column].set(current)
    return result


def upper_solve(factor, target):
    extent = factor.shape[0]
    result = jnp.zeros_like(target)
    for column in reversed(range(extent)):
        current = (target[column] - jnp.sum(factor[:, column] * result, axis=0)) / factor[
            column, column
        ]
        result = result.at[column].set(current)
    return result


def solve_normal(grams, right, modes, rows_all):
    snapshot_count = grams.shape[0]
    identity = jnp.eye(modes, dtype=jnp.float32)[:, :, None]
    system = grams.T.reshape(modes, modes, snapshot_count) + damping * rows_all * identity
    factor = cholesky_last(system)
    return upper_solve(factor, lower_solve(factor, right.T))


def inverse_factor(products):
    extent = products.shape[0]
    factor = cholesky_last(products[:, :, None])
    return lower_solve(factor, jnp.eye(extent, dtype=jnp.float32))


def mask_blocks(samples, flag_blocks):
    snapshot_count, blocks_dev = flag_blocks.shape
    weights = flag_blocks.astype(samples.dtype)[:, :, None]
    return (samples.reshape(snapshot_count, blocks_dev, -1) * weights).reshape(snapshot_count, -1)


def refill(samples, flag_blocks, recon_low):
    snapshot_count, blocks_dev = flag_blocks.shape
    observed = (flag_blocks > 0)[:, :, None]
    combined = jnp.where(
        observed,
        samples.reshape(snapshot_count, blocks_dev, -1),
        recon_low.reshape(snapshot_count, blocks_dev, -1),
    )
    return combined.reshape(snapshot_count, -1)


def contract_rows(former, latter):
    return lax.dot_general(
        former, latter, (((1,), (1,)), ((), ())), preferred_element_type=jnp.float32
    )


def contract_first(former, latter):
    return lax.dot_general(
        former, latter, (((0,), (0,)), ((), ())), preferred_element_type=jnp.float32
    )


def per_device(old_basis, snapshots, gap_flags, sketch_seed):
    modes = old_basis.shape[0]
    rows_all = old_basis.shape[1] * lax.axis_size(("rows", "sub"))
    blocks_dev = gap_flags.shape[1]
    masked = mask_blocks(snapshots, gap_flags)
    right = contract_rows(masked, old_basis)
    pieces = old_basis.reshape(modes, blocks_dev, -1)
    block_grams = jnp.einsum("kbi,lbi->bkl", pieces, pieces, preferred_element_type=jnp.float32)
    block_rows = block_grams.reshape(blocks_dev, modes * modes)
    grams = jnp.dot(gap_flags.astype(jnp.float32), block_rows, precision=highest)
    mixer = sketch_seed.astype(jnp.bfloat16)
    gram_total, right_total = lax.psum((grams, right), ("rows", "sub"))
    coefficients = solve_normal(gram_total, right_total, modes, rows_all)
    recon_low = contract_first(coefficients.astype(jnp.bfloat16), old_basis).astype(jnp.bfloat16)
    filled = refill(snapshots, gap_flags, recon_low)
    sketch = contract_first(mixer, filled)
    inverse = None
    for sweep_index in range(POWER + 1):
        if sweep_index > 0:
            sketch = contract_first(mixer, filled)
        local_gram = lax.dot_general(
            sketch,
            sketch,
            (((1,), (1,)), ((), ())),
            precision=highest,
            preferred_element_type=jnp.float32,
        )
        products = lax.psum(local_gram, ("rows", "sub"))
        inverse = inverse_factor(products)
        if sweep_index < POWER:
            ortho_rows = jnp.dot(inverse, sketch, precision=highest).astype(jnp.bfloat16)
            mixer_share = lax.psum_scatter(
                contract_rows(filled, ortho_rows), ("rows", "sub"), scatter_dimension=0, tiled=True
            ).astype(jnp.bfloat16)
            mixer = lax.all_gather(mixer_share, ("rows", "sub"), axis=0, tiled=True)
    root_rows = math.sqrt(rows_all)
    new_basis = jnp.dot(inverse[:modes], sketch, precision=highest) * root_rows
    return (new_basis, coefficients)


def solution(mesh):
    in_specs = (P(None, ("rows", "sub")), P(None, ("rows", "sub")), P(None, ("rows", "sub")), P())
    out_specs = (P(None, ("rows", "sub")), P())
    return jax.shard_map(
        per_device, mesh=mesh, in_specs=in_specs, out_specs=out_specs, check_vma=False
    )
```

profile of v0, /device:TPU:0, one launch (start us, length us, event | category | flops | bytes accessed | tf_op | source)
XLA Modules:
  0.0 1549.7 jit_solution(17264317991794373059)
XLA Ops:
  11.2 2.8 fusion.6
  16.6 13.0 mul.4308
  29.6 24.4 %fusion.2 = f32[32,512]{1,0:T(8,128)} fusion(bf16[32,16384]{1,0:T(8,128)(2,1)S(1)} %copy-done, bf16[512,16384]{1,0:T(8,128)(2,1)} %param.965, bf16[64,8,128,128]{3,2,1,0:T(8,128)(2,1)} %bitcast.3922), kind=kOutput, calls=%fused_computation.40 | convolution fusion | flops 545259520 | bytes 34668544 | tf_op jit(solution)/shard_map/dot_general | solution.py:78
  54.7 137.0 %all-reduce.12.cloned.1.call-done = (f32[32,32,512]{2,0,1:T(8,128)}, f32[32,512]{1,0:T(8,128)}) async-done(((f32[32,32,512]{2,0,1:T(8,128)}, f32[32,512]{1,0:T(8,128)}), (f32[32,32,512]{2,0,1:T(8,128)}, f32[32,512]{1,0:T(8,128)})) %all-reduce.12.cloned.1.call-update) | async-done | bytes 2162704 | tf_op jit(solution)/shard_map/psum | solution.py:100
  291.6 12.0 broadcast_in_dim.635
  303.5 15.2 bitcast_select_fusion
  318.8 8.8 fusion.224
  329.5 3.4 convolution_bitcast_fusion.2
  332.9 39.6 %psum.37 = f32[64,64,1]{1,0,2:T(8,128)S(1)} all-reduce(f32[64,64,1]{1,0,2:T(8,128)S(1)} %convolution_bitcast_fusion.2), channel_id=1, replica_groups=mesh['rows'=8,'sub'=4] {'rows','sub'}, use_global_device_ids=true, to_apply=%region_97.98 | all-reduce | flops 4096 | bytes 32768 | tf_op jit(solution)/shard_map/psum | solution.py:116
  581.6 6.0 convolution_convert_fusion.2
  587.6 8.8 fusion.526
  596.5 133.4 %reduce-scatter.3.cloned.1.call-done = f32[16,64]{1,0:T(8,128)} async-done(((f32[512,64]{1,0:T(8,128)}), f32[16,64]{1,0:T(8,128)}) %reduce-scatter.3.cloned.1.call-update) | async-done | bytes 4112 | tf_op jit(solution)/shard_map/reduce_scatter | solution.py:120
  730.6 64.8 %all_gather.6 = bf16[512,64]{1,0:T(8,128)(2,1)S(1)} all-gather(bf16[16,64]{1,0:T(8,128)(2,1)S(1)} %convert_element_type.415), channel_id=1, replica_groups=mesh['rows'=8,'sub'=4] {'rows','sub'}, dimensions={0}, use_global_device_ids=true | all-gather | bytes 67584 | tf_op jit(solution)/shard_map/all_gather | solution.py:123
  795.3 8.9 fusion.527
  806.2 3.4 convolution_bitcast_fusion.1
  809.6 39.9 %psum.38 = f32[64,64,1]{1,0,2:T(8,128)S(1)} all-reduce(f32[64,64,1]{1,0,2:T(8,128)S(1)} %convolution_bitcast_fusion.1), channel_id=1, replica_groups=mesh['rows'=8,'sub'=4] {'rows','sub'}, use_global_device_ids=true, to_apply=%region_226.227 | all-reduce | flops 4096 | bytes 32768 | tf_op jit(solution)/shard_map/psum | solution.py:116
  1062.7 6.0 convolution_convert_fusion.1
  1068.7 8.8 fusion.528
  1077.5 133.0 %reduce-scatter.5.cloned.1.call-done = f32[16,64]{1,0:T(8,128)} async-done(((f32[512,64]{1,0:T(8,128)}), f32[16,64]{1,0:T(8,128)}) %reduce-scatter.5.cloned.1.call-update) | async-done | bytes 4112 | tf_op jit(solution)/shard_map/reduce_scatter | solution.py:120
  1211.2 64.8 %all_gather.7 = bf16[512,64]{1,0:T(8,128)(2,1)S(1)} all-gather(bf16[16,64]{1,0:T(8,128)(2,1)S(1)} %convert_element_type.417), channel_id=1, replica_groups=mesh['rows'=8,'sub'=4] {'rows','sub'}, dimensions={0}, use_global_device_ids=true | all-gather | bytes 67584 | tf_op jit(solution)/shard_map/all_gather | solution.py:123
  1276.0 8.9 fusion.529
  1286.8 3.4 convolution_bitcast_fusion
  1290.2 39.9 %psum.39 = f32[64,64,1]{1,0,2:T(8,128)S(1)} all-reduce(f32[64,64,1]{1,0,2:T(8,128)S(1)} %convolution_bitcast_fusion), channel_id=1, replica_groups=mesh['rows'=8,'sub'=4] {'rows','sub'}, use_global_device_ids=true, to_apply=%region_355.356 | all-reduce | flops 4096 | bytes 32768 | tf_op jit(solution)/shard_map/psum | solution.py:116
  1537.1 5.7 convolution_multiply_fusion
  (2342 shorter events, 603.0 us)
Async XLA Ops:
  7.2 1.3 copy-start
  7.2 184.5 %all-reduce.12.cloned.1.call-start = ((), (), s32[]{:S(2)}) async-start(), calls=%async_computation.4 | async-start | bytes 4325376 | tf_op jit(solution)/shard_map/psum | solution.py:100
  9.1 2.1 copy-start.8
  54.0 675.8 %reduce-scatter.3.cloned.1.call-start = ((), (), s32[]{:S(2)}) async-start(), calls=%async_computation.2 | async-start | bytes 270336 | tf_op jit(solution)/shard_map/reduce_scatter | solution.py:120
  54.7 443.3 %copy-start.9 = (f32[64,64]{1,0:T(8,128)}, f32[64,64]{1,0:T(8,128)S(1)}, u32[]{:S(2)}) copy-start(f32[64,64]{1,0:T(8,128)S(1)} %fusion.228) | copy-start | bytes 49156
  210.1 2.8 copy-start.2
  238.2 3.3 copy-start.6
  291.5 12.0 copy-start.7
  303.5 15.2 copy-start.10
  327.5 1.9 copy-start.5
  596.4 614.1 %reduce-scatter.5.cloned.1.call-start = ((), (), s32[]{:S(2)}) async-start(), calls=%async_computation.3 | async-start | bytes 270336 | tf_op jit(solution)/shard_map/reduce_scatter | solution.py:120
  804.2 1.9 copy-start.4
  1284.9 1.9 copy-start.3
  1537.0 5.7 copy-start.1
Sparse Core Ops, SparseCore 0:
  54.2 137.4 all-reduce.11
  596.5 133.2 reduce-scatter.2
  1077.6 132.8 reduce-scatter.4
where the time goes:
time: 1580 us; the launch traced here: 1550 us
  waiting for transfers between devices  403 us (26%)
  other arithmetic  392 us (25%)
  blocking collectives  249 us (16%)
  local copies, waits for them, and re-layouts  234 us (15%)
  between operations  155 us (10%)
  matrix products  115 us (7%)
    div x219, other arithmetic, lower_solve(): (target[column] - jnp.sum(factor[column] * result, axis=0)) / factor[colu...  267 us
    reduce_scatter x2, waiting for transfers between devices, per_device(): lax.psum_scatter(contract_rows(filled, ortho_rows), ('rows', 'sub'), scat...  266 us
    psum x1, waiting for transfers between devices, per_device(): gram_total, right_total = lax.psum((grams, right), ('rows', 'sub'))  137 us
    all_gather x2, blocking collectives, per_device(): mixer = lax.all_gather(mixer_share, ('rows', 'sub'), axis=0, tiled=True)  130 us
    psum x3, blocking collectives, per_device(): products = lax.psum(local_gram, ('rows', 'sub'))  119 us
    slice x192, local copies, waits for them, and re-layouts, cholesky_last(): diagonal_root = jnp.sqrt(remain[column])  113 us
    dot_general x3, matrix products, contract_rows(): lax.dot_general(former, latter, (((1,), (1,)), ((), ())), preferred_eleme...  42 us
    dot_general x4, matrix products, contract_first(): lax.dot_general(former, latter, (((0,), (0,)), ((), ())), preferred_eleme...  41.8 us
  transfers between devices with their start and end apart: 3, of which 3 were waited for; matrix products, arithmetic and copies ran while one was open for 0% of the time, Pallas kernels for 0%

commit v1 on v0

--- a/solution.py
+++ b/solution.py
@@ -3,10 +3,15 @@
 import jax.numpy as jnp
 from jax import lax
 from jax.sharding import PartitionSpec as P
+from jax.lax import all_gather
 
 POWER = 2
 damping = 0.005
 highest = lax.Precision.HIGHEST
+
+
+def _push_plate(xx, peer_axis):
+    return jnp.sum(all_gather(xx, peer_axis), axis=0)
 
 
 def cholesky_last(system):
@@ -113,7 +118,7 @@
             precision=highest,
             preferred_element_type=jnp.float32,
         )
-        products = lax.psum(local_gram, ("rows", "sub"))
+        products = _push_plate(local_gram, ("rows", "sub"))
         inverse = inverse_factor(products)
         if sweep_index < POWER:
             ortho_rows = jnp.dot(inverse, sketch, precision=highest).astype(jnp.bfloat16)

time: 1580 us -> 1670 us (1.057)
  blocking collectives: 249 us -> 353 us
    all_gather x0 -> x3, blocking collectives: none -> 224 us  [_push_plate(): return jnp.sum(all_gather(xx, peer_axis), axis=0)]
    psum x3 -> x0, blocking collectives: 119 us -> none  [per_device(): products = lax.psum(local_gram, ('rows', 'sub'))]
where the time goes in v1:
time: 1670 us; the launch traced here: 1640 us
  waiting for transfers between devices  399 us (24%)
  other arithmetic  393 us (24%)
  blocking collectives  353 us (21%)
  local copies, waits for them, and re-layouts  229 us (14%)
  between operations  155 us (9%)
  matrix products  115 us (7%)
    div x219, other arithmetic, lower_solve(): (target[column] - jnp.sum(factor[column] * result, axis=0)) / factor[colu...  267 us
    reduce_scatter x2, waiting for transfers between devices, per_device(): lax.psum_scatter(contract_rows(filled, ortho_rows), ('rows', 'sub'), scat...  262 us
    all_gather x3, blocking collectives, _push_plate(): return jnp.sum(all_gather(xx, peer_axis), axis=0)  224 us
    psum x1, waiting for transfers between devices, per_device(): gram_total, right_total = lax.psum((grams, right), ('rows', 'sub'))  137 us
    all_gather x2, blocking collectives, per_device(): mixer = lax.all_gather(mixer_share, ('rows', 'sub'), axis=0, tiled=True)  130 us
    slice x192, local copies, waits for them, and re-layouts, cholesky_last(): diagonal_root = jnp.sqrt(remain[column])  113 us
    dot_general x3, matrix products, contract_rows(): lax.dot_general(former, latter, (((1,), (1,)), ((), ())), preferred_eleme...  42 us
    dot_general x4, matrix products, contract_first(): lax.dot_general(former, latter, (((0,), (0,)), ((), ())), preferred_eleme...  41.8 us
  transfers between devices with their start and end apart: 3, of which 3 were waited for; matrix products, arithmetic and copies ran while one was open for 0% of the time, Pallas kernels for 0%

profile of v1, /device:TPU:0, one launch (start us, length us, event | category | flops | bytes accessed | tf_op | source)
XLA Modules:
  0.0 1644.3 jit_solution(8783778420193226714)
XLA Ops:
  11.2 2.8 fusion.6
  16.6 13.0 mul.4308
  29.6 24.4 %fusion.2 = f32[32,512]{1,0:T(8,128)} fusion(bf16[32,16384]{1,0:T(8,128)(2,1)S(1)} %copy-done, bf16[512,16384]{1,0:T(8,128)(2,1)} %param.965, bf16[64,8,128,128]{3,2,1,0:T(8,128)(2,1)} %bitcast.4126), kind=kOutput, calls=%fused_computation.40 | convolution fusion | flops 545259520 | bytes 34668544 | tf_op jit(solution)/shard_map/dot_general | solution.py:83
  54.7 137.0 %all-reduce.12.cloned.1.call-done = (f32[32,32,512]{2,0,1:T(8,128)}, f32[32,512]{1,0:T(8,128)}) async-done(((f32[32,32,512]{2,0,1:T(8,128)}, f32[32,512]{1,0:T(8,128)}), (f32[32,32,512]{2,0,1:T(8,128)}, f32[32,512]{1,0:T(8,128)})) %all-reduce.12.cloned.1.call-update) | async-done | bytes 2162704 | tf_op jit(solution)/shard_map/psum | solution.py:105
  291.5 12.0 broadcast_in_dim.635
  303.5 15.2 bitcast_select_fusion
  318.6 8.8 fusion.224
  327.4 3.4 fusion.526
  330.8 75.7 %all-gather = f32[2048,64]{1,0:T(8,128)S(1)} all-gather(f32[64,64]{1,0:T(8,128)S(1)} %fusion.526), channel_id=2, replica_groups=mesh['rows'=8,'sub'=4] {'rows','sub'}, dimensions={0}, use_global_device_ids=true | all-gather | bytes 540672 | tf_op jit(solution)/shard_map/all_gather | solution.py:14
  615.8 6.0 convolution_convert_fusion.2
  621.8 8.8 fusion.527
  630.7 131.0 %reduce-scatter.3.cloned.1.call-done = f32[16,64]{1,0:T(8,128)} async-done(((f32[512,64]{1,0:T(8,128)}), f32[16,64]{1,0:T(8,128)}) %reduce-scatter.3.cloned.1.call-update) | async-done | bytes 4112 | tf_op jit(solution)/shard_map/reduce_scatter | solution.py:125
  762.4 64.8 %all_gather.26 = bf16[512,64]{1,0:T(8,128)(2,1)S(1)} all-gather(bf16[16,64]{1,0:T(8,128)(2,1)S(1)} %convert_element_type.415), channel_id=1, replica_groups=mesh['rows'=8,'sub'=4] {'rows','sub'}, dimensions={0}, use_global_device_ids=true | all-gather | bytes 67584 | tf_op jit(solution)/shard_map/all_gather | solution.py:128
  827.2 8.9 fusion.528
  836.1 3.4 fusion.529
  839.5 74.1 %all-gather.1 = f32[2048,64]{1,0:T(8,128)S(1)} all-gather(f32[64,64]{1,0:T(8,128)S(1)} %fusion.529), channel_id=3, replica_groups=mesh['rows'=8,'sub'=4] {'rows','sub'}, dimensions={0}, use_global_device_ids=true | all-gather | bytes 540672 | tf_op jit(solution)/shard_map/all_gather | solution.py:14
  1126.9 6.0 convolution_convert_fusion.1
  1132.9 8.8 fusion.530
  1141.7 131.0 %reduce-scatter.5.cloned.1.call-done = f32[16,64]{1,0:T(8,128)} async-done(((f32[512,64]{1,0:T(8,128)}), f32[16,64]{1,0:T(8,128)}) %reduce-scatter.5.cloned.1.call-update) | async-done | bytes 4112 | tf_op jit(solution)/shard_map/reduce_scatter | solution.py:125
  1273.4 64.7 %all_gather.29 = bf16[512,64]{1,0:T(8,128)(2,1)S(1)} all-gather(bf16[16,64]{1,0:T(8,128)(2,1)S(1)} %convert_element_type.417), channel_id=1, replica_groups=mesh['rows'=8,'sub'=4] {'rows','sub'}, dimensions={0}, use_global_device_ids=true | all-gather | bytes 67584 | tf_op jit(solution)/shard_map/all_gather | solution.py:128
  1338.1 8.9 fusion.531
  1347.1 3.4 fusion.532
  1350.5 74.1 %all-gather.2 = f32[2048,64]{1,0:T(8,128)S(1)} all-gather(f32[64,64]{1,0:T(8,128)S(1)} %fusion.532), channel_id=4, replica_groups=mesh['rows'=8,'sub'=4] {'rows','sub'}, dimensions={0}, use_global_device_ids=true | all-gather | bytes 540672 | tf_op jit(solution)/shard_map/all_gather | solution.py:14
  1631.6 5.7 convolution_multiply_fusion
  (2345 shorter events, 597.4 us)
Async XLA Ops:
  7.2 1.3 copy-start
  7.2 184.5 %all-reduce.12.cloned.1.call-start = ((), (), s32[]{:S(2)}) async-start(), calls=%async_computation.4 | async-start | bytes 4325376 | tf_op jit(solution)/shard_map/psum | solution.py:105
  9.1 2.1 copy-start.8
  54.0 707.6 %reduce-scatter.3.cloned.1.call-start = ((), (), s32[]{:S(2)}) async-start(), calls=%async_computation.2 | async-start | bytes 270336 | tf_op jit(solution)/shard_map/reduce_scatter | solution.py:125
  54.7 477.5 %copy-start.9 = (f32[64,64]{1,0:T(8,128)}, f32[64,64]{1,0:T(8,128)S(1)}, u32[]{:S(2)}) copy-start(f32[64,64]{1,0:T(8,128)S(1)} %fusion.228) | copy-start | bytes 49156
  210.0 2.8 copy-start.2
  238.1 3.3 copy-start.6
  291.5 12.0 copy-start.7
  303.5 15.2 copy-start.10
  327.4 3.4 copy-start.5
  630.6 642.1 %reduce-scatter.5.cloned.1.call-start = ((), (), s32[]{:S(2)}) async-start(), calls=%async_computation.3 | async-start | bytes 270336 | tf_op jit(solution)/shard_map/reduce_scatter | solution.py:125
  836.1 3.4 copy-start.4
  1347.1 3.4 copy-start.3
  1631.6 5.7 copy-start.1
Sparse Core Ops, SparseCore 0:
  54.2 137.4 all-reduce.11
  630.7 130.9 reduce-scatter.2
  1141.9 130.8 reduce-scatter.4
